TPU v7x, 512 devices: a whole 4x8x8 slice. The times are simulated.
512 devices in a mesh: row: 16 (over y_hi, z), col: 32 (over y_lo, x, core).
Axes of the slice: x: 4, y: 8 (y_hi: 2, y_lo: 4; y = y_hi * 4 + y_lo), z: 8, core: 2. Of those that a mesh axis runs over, the one named last changes fastest.
Arguments:
- features: bfloat16 [65536, 256], P(('col', 'row')), may hold values from -6 to 6
- weight: bfloat16 [256, 256], replicated, may hold values from -0.375 to 0.375
- bias: float32 [256], replicated, may hold values from -3 to 3
- grad_out: bfloat16 [65536, 256], P(('row', 'col')), may hold values from -6 to 6
- tile_rows: int32 [16, 32, 128], P('row', 'col'), may hold values from 0 to 31
- tile_cols: int32 [16, 32, 128], P('row', 'col'), may hold values from 0 to 15
- tile_counts: int32 [16, 32], P('row', 'col'), may hold values from 1 to 128, as said below
- tile_values: bfloat16 [16, 32, 128, 128, 128], P('row', 'col'), may hold values from 0 to 0.011962891
Outputs:
- output: bfloat16 [65536, 256], P(('row', 'col'))
- grad_features: bfloat16 [65536, 256], P(('col', 'row'))
- grad_weight: float32 [256, 256], replicated
- grad_bias: float32 [256], replicated
Inputs may be any that keep to these rules, and one draw needn't show every extreme that they name: `tile_counts`: some grid cell has all 128 slots live. Tile coordinates may repeat within a cell; repeated tiles add.
All inputs are finite; a program needn't handle non-finite values.
Results may differ from a plain program's by a relative error of at most 0.018.
Values may be sent and summed in bfloat16 or wider, within the bound.
No kernel may reach another device: no remote copies, remote signals or barrier semaphores. Data moves between devices by JAX's collectives and lax.ppermute only.
A program may use at most 64 MiB of HBM per device.

v0:
```python
import jax
import jax.numpy as jnp
from jax import lax
from jax.sharding import PartitionSpec as P

GROUP = 8


def elu_value(pre):
    return jnp.where(pre > 0, pre, jnp.expm1(jnp.minimum(pre, 0.0)))


def elu_slope(pre):
    return jnp.where(pre > 0, jnp.float32(1.0), jnp.exp(jnp.minimum(pre, 0.0)))


def accumulate(values, dest_idx, src_idx, live, source, dest_tiles, transpose):
    side = values.shape[-1]
    width = source.shape[-1]
    group_size = GROUP
    blocks_all = source.reshape(source.shape[0] // side, side, width)

    def one_group(step, acc):
        first = step * group_size
        part_values = lax.dynamic_slice_in_dim(values, first, group_size, 0)
        part_dest = lax.dynamic_slice_in_dim(dest_idx, first, group_size, 0)
        part_src = lax.dynamic_slice_in_dim(src_idx, first, group_size, 0)
        blocks = jnp.take(blocks_all, part_src, axis=0)
        if transpose:
            prod = jnp.einsum(
                "gab,gac->gbc", part_values, blocks, preferred_element_type=jnp.float32
            )
        else:
            prod = jnp.einsum(
                "gab,gbc->gac", part_values, blocks, preferred_element_type=jnp.float32
            )
        keep = (jnp.arange(group_size) + first < live).astype(jnp.float32)
        return acc.at[part_dest].add(prod * keep[:, None, None])

    start_acc = jnp.zeros((dest_tiles, side, width), jnp.float32)
    steps_used = values.shape[0] // group_size
    total = lax.fori_loop(0, steps_used, one_group, start_acc)
    return total.reshape(dest_tiles * side, width)


def body(features, weight, bias, grad_out, tile_rows, tile_cols, tile_counts, tile_values):
    values = tile_values[0, 0]
    rows_idx = tile_rows[0, 0]
    cols_idx = tile_cols[0, 0]
    live = tile_counts[0, 0]
    side = values.shape[-1]
    share = features.shape[0]
    row_tiles = share * lax.axis_size("col") // side
    col_tiles = share * lax.axis_size("row") // side
    mixed = jnp.dot(features, weight, preferred_element_type=jnp.float32).astype(jnp.bfloat16)
    column_block = lax.all_gather(mixed, "row", axis=0, tiled=True)
    partial_value = accumulate(values, rows_idx, cols_idx, live, column_block, row_tiles, False)
    pre_share = (
        lax.psum_scatter(
            partial_value.astype(jnp.bfloat16), "col", scatter_dimension=0, tiled=True
        ).astype(jnp.float32)
        + bias[None, :]
    )
    grad_share = (grad_out.astype(jnp.float32) * elu_slope(pre_share)).astype(jnp.bfloat16)
    grad_block = lax.all_gather(grad_share, "col", axis=0, tiled=True)
    output = elu_value(pre_share).astype(jnp.bfloat16)
    back = accumulate(values, cols_idx, rows_idx, live, grad_block, col_tiles, True)
    grad_mixed = lax.psum_scatter(back.astype(jnp.bfloat16), "row", scatter_dimension=0, tiled=True)
    grad_features = lax.dot_general(
        grad_mixed, weight, (((1,), (1,)), ((), ())), preferred_element_type=jnp.float32
    ).astype(jnp.bfloat16)
    weight_term = lax.dot_general(
        features, grad_mixed, (((0,), (0,)), ((), ())), preferred_element_type=jnp.float32
    )
    bias_term = jnp.sum(grad_share.astype(jnp.float32), axis=0)
    grad_weight, grad_bias = lax.psum((weight_term, bias_term), ("row", "col"))
    return (output, grad_features, grad_weight, grad_bias)


def solution(mesh):
    placed = (
        P(("col", "row"), None),
        P(),
        P(),
        P(("row", "col"), None),
        P("row", "col", None),
        P("row", "col", None),
        P("row", "col"),
        P("row", "col", None, None, None),
    )
    return jax.shard_map(
        body,
        mesh=mesh,
        in_specs=placed,
        out_specs=(P(("row", "col"), None), P(("col", "row"), None), P(), P()),
        check_vma=False,
    )
```

profile of v0, /device:TPU:23, one launch (start us, length us, event | category | flops | bytes accessed | tf_op | source)
XLA Modules:
  0.0 1037.7 jit_solution(1046019565683276147)
XLA Ops:
  8.1 1.6 convolution_convert_fusion.1
  9.8 93.5 %all-gather.3.cloned.1.call-done = bf16[2048,256]{1,0:T(8,128)(2,1)} async-done(((bf16[128,256]{1,0:T(8,128)(2,1)}), bf16[2048,256]{1,0:T(8,128)(2,1)}) %all-gather.3.cloned.1.call-update) | async-done | bytes 1048592 | tf_op jit(solution)/shard_map/all_gather | solution.py:56
  103.3 2.4 broadcast_in_dim.79
  105.7 96.6 %while.26 = (s32[]{:T(128)}, f32[32,128,256]{2,1,0:T(8,128)}, s32[128]{0:T(128)S(1)}, bf16[128,128,128]{2,1,0:T(8,128)(2,1)}, s32[128]{0:T(128)S(1)}, /*index=5*...) while((s32[]{:T(128)}, f32[32,128,256]{2,1,0:T(8,128)}, ...), condition=%wide.region_2.3_spmd, body=%wide.region_0.2_spmd.sunk | while | flops 67896424 | bytes 6033887 | solution.py:42
  108.4 3.3 scatter_fusion
  114.5 3.3 scatter_fusion
  120.6 3.3 scatter_fusion
  126.6 3.3 scatter_fusion
  132.7 3.2 scatter_fusion
  138.6 3.3 scatter_fusion
  144.6 3.3 scatter_fusion
  150.6 3.3 scatter_fusion
  156.7 3.2 scatter_fusion
  162.7 3.3 scatter_fusion
  168.7 3.3 scatter_fusion
  174.7 3.3 scatter_fusion
  180.8 3.3 scatter_fusion
  186.8 3.4 scatter_fusion
  192.9 3.4 scatter_fusion
  199.0 3.3 scatter_fusion
  202.3 3.8 convert_element_type.56
  206.2 125.6 %reduce-scatter.3.cloned.1.call-done = bf16[128,256]{1,0:T(8,128)(2,1)} async-done(((bf16[4096,256]{1,0:T(8,128)(2,1)}), bf16[128,256]{1,0:T(8,128)(2,1)}) %reduce-scatter.3.cloned.1.call-update) | async-done | bytes 65552 | tf_op jit(solution)/shard_map/reduce_scatter | solution.py:59
  333.5 6.4 copy.12
  339.9 75.5 %all-gather.5.cloned.1.call-done = bf16[4096,256]{1,0:T(8,128)(2,1)} async-done(((bf16[128,256]{1,0:T(8,128)(2,1)}), bf16[4096,256]{1,0:T(8,128)(2,1)}) %all-gather.5.cloned.1.call-update) | async-done | bytes 2097168 | tf_op jit(solution)/shard_map/all_gather | solution.py:65
  417.0 121.8 %while.27 = (s32[]{:T(128)}, f32[16,128,256]{2,1,0:T(8,128)}, s32[128]{0:T(128)S(1)}, bf16[128,128,128]{1,2,0:T(8,128)(2,1)}, s32[128]{0:T(128)S(1)}, /*index=5*...) while((s32[]{:T(128)}, f32[16,128,256]{2,1,0:T(8,128)}, ...), condition=%wide.region_6.7_spmd, body=%wide.region_4.6_spmd.sunk | while | flops 67896424 | bytes 6033887 | solution.py:42
  417.7 2.2 gather_fusion.1
  421.3 3.3 scatter_fusion.1
  425.3 2.2 gather_fusion.1
  428.9 3.3 scatter_fusion.1
  433.0 2.2 gather_fusion.1
  436.6 3.3 scatter_fusion.1
  440.6 2.2 gather_fusion.1
  444.2 3.3 scatter_fusion.1
  448.3 2.2 gather_fusion.1
  451.9 3.3 scatter_fusion.1
  455.8 2.2 gather_fusion.1
  459.4 3.3 scatter_fusion.1
  463.5 2.2 gather_fusion.1
  467.0 3.3 scatter_fusion.1
  471.1 2.2 gather_fusion.1
  474.6 3.3 scatter_fusion.1
  478.7 2.2 gather_fusion.1
  482.3 3.3 scatter_fusion.1
  486.3 2.2 gather_fusion.1
  489.9 3.3 scatter_fusion.1
  493.9 2.2 gather_fusion.1
  497.5 3.3 scatter_fusion.1
  501.5 2.2 gather_fusion.1
  505.1 3.3 scatter_fusion.1
  509.1 2.2 gather_fusion.1
  512.7 3.3 scatter_fusion.1
  516.7 2.2 gather_fusion.1
  520.3 3.3 scatter_fusion.1
  524.3 2.2 gather_fusion.1
  527.9 3.3 scatter_fusion.1
  532.0 2.2 gather_fusion.1
  535.6 3.3 scatter_fusion.1
  538.8 2.7 convert_element_type.62
  541.6 97.9 %psum.15 = f32[256]{0:T(256)} all-reduce(f32[256]{0:T(256)S(1)} %get-tuple-element.297), channel_id=1, replica_groups=mesh['row'=16,'col'=32] {'row','col'}, use_global_device_ids=true, to_apply=%region_10.11 | all-reduce | flops 256 | bytes 2048 | tf_op jit(solution)/shard_map/psum | solution.py:76
  639.5 113.2 %reduce-scatter.5.cloned.1.call-done = bf16[128,256]{1,0:T(8,128)(2,1)} async-done(((bf16[2048,256]{1,0:T(8,128)(2,1)}), bf16[128,256]{1,0:T(8,128)(2,1)}) %reduce-scatter.5.cloned.1.call-update) | async-done | bytes 65552 | tf_op jit(solution)/shard_map/reduce_scatter | solution.py:68
  752.7 1.8 convolution_bitcast_fusion
  754.5 1.7 convolution_convert_fusion
  756.2 273.2 %all-reduce.2.cloned.1.call-done = f32[256,256]{0,1:T(8,128)} async-done(((f32[256,256]{0,1:T(8,128)}), f32[256,256]{0,1:T(8,128)}) %all-reduce.2.cloned.1.call-update) | async-done | bytes 262160 | tf_op jit(solution)/shard_map/psum | solution.py:76
  1029.4 1.8 copy.14
  (170 shorter events, 81.8 us)
Async XLA Ops:
  7.2 0.9 copy-start
  7.2 98.5 %copy-start.4 = (s32[1,1,128]{2,1,0:T(1,128)S(1)}, s32[1,1,128]{2,1,0:T(1,128)}, u32[]{:S(2)}) copy-start(s32[1,1,128]{2,1,0:T(1,128)} %param.16) | copy-start | bytes 1540
  7.2 98.5 %copy-start.5 = (s32[1,1,128]{2,1,0:T(1,128)S(1)}, s32[1,1,128]{2,1,0:T(1,128)}, u32[]{:S(2)}) copy-start(s32[1,1,128]{2,1,0:T(1,128)} %param.17) | copy-start | bytes 1540
  7.2 96.1 %all-gather.3.cloned.1.call-start = ((), (), s32[]{:S(2)}) async-start(), calls=%async_computation.2 | async-start | bytes 1114112 | tf_op jit(solution)/shard_map/all_gather | solution.py:56
  9.7 322.1 %reduce-scatter.3.cloned.1.call-start = ((), (), s32[]{:S(2)}) async-start(), calls=%async_computation.3 | async-start | bytes 2162688 | tf_op jit(solution)/shard_map/reduce_scatter | solution.py:59
  103.3 2.4 copy-start.1
  202.3 129.6 %copy-start.3 = (bf16[128,256]{1,0:T(8,128)(2,1)S(1)}, bf16[128,256]{1,0:T(8,128)(2,1)}, u32[]{:S(2)}) copy-start(bf16[128,256]{1,0:T(8,128)(2,1)} %param.15) | copy-start | bytes 196612
  202.3 129.6 %copy-start.6 = (f32[256]{0:T(256)S(1)}, f32[256]{0:T(256)}, u32[]{:S(2)}) copy-start(f32[256]{0:T(256)} %param.14) | copy-start | bytes 3076
  206.1 209.3 %all-gather.5.cloned.1.call-start = ((), (), s32[]{:S(2)}) async-start(), calls=%async_computation.4 | async-start | bytes 2162688 | tf_op jit(solution)/shard_map/all_gather | solution.py:65
  333.4 419.3 %reduce-scatter.5.cloned.1.call-start = ((), (), s32[]{:S(2)}) async-start(), calls=%async_computation.5 | async-start | bytes 1114112 | tf_op jit(solution)/shard_map/reduce_scatter | solution.py:68
  538.8 213.9 %copy-start.2 = (bf16[128,256]{1,0:T(8,128)(2,1)S(1)}, bf16[128,256]{1,0:T(8,128)(2,1)}, u32[]{:S(2)}) copy-start(bf16[128,256]{1,0:T(8,128)(2,1)} %param.12) | copy-start | bytes 196612
  541.6 487.8 %all-reduce.2.cloned.1.call-start = ((), (), s32[]{:S(2)}) async-start(), calls=%async_computation.6 | async-start | bytes 524288 | tf_op jit(solution)/shard_map/psum | solution.py:76
Sparse Core Ops, SparseCore 0:
  11.8 91.4 all-gather.2
  206.3 125.5 reduce-scatter.2
  334.8 80.5 all-gather.4
  541.7 210.9 reduce-scatter.4
  758.9 270.4 all-reduce.1
where the time goes:
time: 1040 us
  waiting for transfers between devices  681 us (65%)
  other arithmetic  140 us (13%)
  blocking collectives  97.9 us (9%)
  local copies, waits for them, and re-layouts  57 us (5%)
  matrix products  47.3 us (5%)
  between operations  13.8 us (1%)
    psum x1, waiting for transfers between devices, body(): grad_weight, grad_bias = lax.psum((weight_term, bias_term), ('row', 'col'))  273 us
    reduce_scatter x1, waiting for transfers between devices, body(): lax.psum_scatter(partial_value.astype(jnp.bfloat16), 'col', scatter_dimen...  126 us
    reduce_scatter x1, waiting for transfers between devices, body(): lax.psum_scatter(back.astype(jnp.bfloat16), 'row', scatter_dimension=0, t...  113 us
    scatter-add x32, other arithmetic, one_group(): return acc.at[part_dest].add(prod * keep[:, None, None])  106 us
    psum x1, blocking collectives, body(): grad_weight, grad_bias = lax.psum((weight_term, bias_term), ('row', 'col'))  97.9 us
    all_gather x1, waiting for transfers between devices, body(): column_block = lax.all_gather(mixed, 'row', axis=0, tiled=True)  93.5 us
    all_gather x1, waiting for transfers between devices, body(): grad_block = lax.all_gather(grad_share, 'col', axis=0, tiled=True)  75.5 us
    gather x32, local copies, waits for them, and re-layouts, one_group(): blocks = jnp.take(blocks_all, part_src, axis=0)  44 us
  transfers between devices with their start and end apart: 5, of which 5 were waited for; matrix products, arithmetic and copies ran while one was open for 1% of the time, Pallas kernels for 0%

commit v1 on v0

--- a/solution.py
+++ b/solution.py
@@ -73,7 +73,7 @@
         features, grad_mixed, (((0,), (0,)), ((), ())), preferred_element_type=jnp.float32
     )
     bias_term = jnp.sum(grad_share.astype(jnp.float32), axis=0)
-    grad_weight, grad_bias = lax.psum((weight_term, bias_term), ("row", "col"))
+    grad_weight, grad_bias = lax.psum(lax.psum((weight_term, bias_term), "row"), "col")
     return (output, grad_features, grad_weight, grad_bias)
 
 

time: 1040 us -> 1250 us (1.20)
  the two profiles are of different devices: /device:TPU:23 before, /device:TPU:1 now
where the time goes in v1:
time: 1250 us; the launch traced here: 1240 us
  waiting for transfers between devices  852 us (68%)
  other arithmetic  139 us (11%)
  blocking collectives  132 us (11%)
  local copies, waits for them, and re-layouts  57 us (5%)
  matrix products  47.3 us (4%)
  between operations  14.1 us (1%)
    reduce_scatter x1, waiting for transfers between devices, body(): lax.psum_scatter(back.astype(jnp.bfloat16), 'row', scatter_dimension=0, t...  211 us
    psum x1, waiting for transfers between devices, body(): lax.psum((weight_term, bias_term), 'row')  187 us
    psum x1, waiting for transfers between devices, body(): lax.psum(lax.psum((weight_term, bias_term), 'row'), 'col')  156 us
    reduce_scatter x1, waiting for transfers between devices, body(): lax.psum_scatter(partial_value.astype(jnp.bfloat16), 'col', scatter_dimen...  146 us
    scatter-add x32, other arithmetic, one_group(): return acc.at[part_dest].add(prod * keep[:, None, None])  105 us
    all_gather x1, waiting for transfers between devices, body(): column_block = lax.all_gather(mixed, 'row', axis=0, tiled=True)  92.8 us
    psum x1, blocking collectives, body(): lax.psum(lax.psum((weight_term, bias_term), 'row'), 'col')  85.9 us
    all_gather x1, waiting for transfers between devices, body(): grad_block = lax.all_gather(grad_share, 'col', axis=0, tiled=True)  58.6 us
  transfers between devices with their start and end apart: 6, of which 6 were waited for; matrix products, arithmetic and copies ran while one was open for 1% of the time, Pallas kernels for 0%

profile of v1, /device:TPU:1, one launch (start us, length us, event | category | flops | bytes accessed | tf_op | source)
XLA Modules:
  0.0 1242.3 jit_solution(4216942000139549076)
XLA Ops:
  9.8 92.8 %all-gather.3.cloned.1.call-done = bf16[2048,256]{1,0:T(8,128)(2,1)} async-done(((bf16[128,256]{1,0:T(8,128)(2,1)}), bf16[2048,256]{1,0:T(8,128)(2,1)}) %all-gather.3.cloned.1.call-update) | async-done | bytes 1048592 | tf_op jit(solution)/shard_map/all_gather | solution.py:56
  102.5 2.4 broadcast_in_dim.79
  105.0 96.4 %while.26 = (s32[]{:T(128)}, f32[32,128,256]{2,1,0:T(8,128)}, s32[128]{0:T(128)S(1)}, bf16[128,128,128]{2,1,0:T(8,128)(2,1)}, s32[128]{0:T(128)S(1)}, /*index=5*...) while((s32[]{:T(128)}, f32[32,128,256]{2,1,0:T(8,128)}, ...), condition=%wide.region_2.3_spmd, body=%wide.region_0.2_spmd.sunk | while | flops 67896424 | bytes 6033887 | solution.py:42
  107.7 3.3 scatter_fusion
  113.8 3.3 scatter_fusion
  119.8 3.3 scatter_fusion
  125.9 3.3 scatter_fusion
  131.9 3.3 scatter_fusion
  138.0 3.3 scatter_fusion
  144.0 3.3 scatter_fusion
  150.0 3.3 scatter_fusion
  156.1 3.2 scatter_fusion
  162.0 3.3 scatter_fusion
  168.0 3.3 scatter_fusion
  174.1 3.3 scatter_fusion
  180.1 3.3 scatter_fusion
  186.1 3.3 scatter_fusion
  192.1 3.3 scatter_fusion
  198.1 3.3 scatter_fusion
  201.4 3.8 convert_element_type.56
  205.3 146.1 %reduce-scatter.3.cloned.1.call-done = bf16[128,256]{1,0:T(8,128)(2,1)} async-done(((bf16[4096,256]{1,0:T(8,128)(2,1)}), bf16[128,256]{1,0:T(8,128)(2,1)}) %reduce-scatter.3.cloned.1.call-update) | async-done | bytes 65552 | tf_op jit(solution)/shard_map/reduce_scatter | solution.py:59
  353.1 6.4 copy.12
  359.5 58.6 %all-gather.5.cloned.1.call-done = bf16[4096,256]{1,0:T(8,128)(2,1)} async-done(((bf16[128,256]{1,0:T(8,128)(2,1)}), bf16[4096,256]{1,0:T(8,128)(2,1)}) %all-gather.5.cloned.1.call-update) | async-done | bytes 2097168 | tf_op jit(solution)/shard_map/all_gather | solution.py:65
  419.7 121.8 %while.27 = (s32[]{:T(128)}, f32[16,128,256]{2,1,0:T(8,128)}, s32[128]{0:T(128)S(1)}, bf16[128,128,128]{1,2,0:T(8,128)(2,1)}, s32[128]{0:T(128)S(1)}, /*index=5*...) while((s32[]{:T(128)}, f32[16,128,256]{2,1,0:T(8,128)}, ...), condition=%wide.region_6.7_spmd, body=%wide.region_4.6_spmd.sunk | while | flops 67896424 | bytes 6033887 | solution.py:42
  420.4 2.2 gather_fusion.1
  424.0 3.2 scatter_fusion.1
  428.0 2.2 gather_fusion.1
  431.6 3.3 scatter_fusion.1
  435.6 2.2 gather_fusion.1
  439.2 3.3 scatter_fusion.1
  443.3 2.2 gather_fusion.1
  446.9 3.3 scatter_fusion.1
  450.9 2.2 gather_fusion.1
  454.5 3.3 scatter_fusion.1
  458.5 2.2 gather_fusion.1
  462.1 3.3 scatter_fusion.1
  466.2 2.2 gather_fusion.1
  469.8 3.3 scatter_fusion.1
  473.9 2.2 gather_fusion.1
  477.4 3.2 scatter_fusion.1
  481.4 2.2 gather_fusion.1
  485.0 3.3 scatter_fusion.1
  489.0 2.2 gather_fusion.1
  492.6 3.3 scatter_fusion.1
  496.6 2.2 gather_fusion.1
  500.2 3.2 scatter_fusion.1
  504.2 2.2 gather_fusion.1
  507.7 3.2 scatter_fusion.1
  511.7 2.2 gather_fusion.1
  515.3 3.3 scatter_fusion.1
  519.3 2.2 gather_fusion.1
  522.9 3.3 scatter_fusion.1
  526.9 2.2 gather_fusion.1
  530.5 3.3 scatter_fusion.1
  534.6 2.2 gather_fusion.1
  538.2 3.3 scatter_fusion.1
  541.5 2.7 convert_element_type.62
  544.2 211.2 %reduce-scatter.5.cloned.1.call-done = bf16[128,256]{1,0:T(8,128)(2,1)} async-done(((bf16[2048,256]{1,0:T(8,128)(2,1)}), bf16[128,256]{1,0:T(8,128)(2,1)}) %reduce-scatter.5.cloned.1.call-update) | async-done | bytes 65552 | tf_op jit(solution)/shard_map/reduce_scatter | solution.py:68
  755.4 1.8 convolution_bitcast_fusion
  757.3 186.7 %all-reduce.3.cloned.1.call-done = f32[256,256]{0,1:T(8,128)} async-done(((f32[256,256]{0,1:T(8,128)}), f32[256,256]{0,1:T(8,128)}) %all-reduce.3.cloned.1.call-update) | async-done | bytes 262160 | tf_op jit(solution)/shard_map/psum | solution.py:76
  944.0 45.7 %psum.30 = f32[256]{0:T(256)S(1)} all-reduce(f32[256]{0:T(256)S(1)} %get-tuple-element.297), channel_id=1, replica_groups=mesh['row'=16,'col'=32] {'row'}, use_global_device_ids=true, to_apply=%region_11.12 | all-reduce | flops 256 | bytes 2048 | tf_op jit(solution)/shard_map/psum | solution.py:76
  989.7 85.9 %psum.31 = f32[256]{0:T(256)} all-reduce(f32[256]{0:T(256)S(1)} %psum.30), channel_id=1, replica_groups=mesh['row'=16,'col'=32] {'col'}, use_global_device_ids=true, to_apply=%region_12.13 | all-reduce | flops 256 | bytes 2048 | tf_op jit(solution)/shard_map/psum | solution.py:76
  1077.3 156.4 %all-reduce.5.cloned.1.call-done = f32[256,256]{0,1:T(8,128)} async-done(((f32[256,256]{0,1:T(8,128)}), f32[256,256]{0,1:T(8,128)}) %all-reduce.5.cloned.1.call-update) | async-done | bytes 262160 | tf_op jit(solution)/shard_map/psum | solution.py:76
  1233.7 1.8 copy.14
  (174 shorter events, 85.1 us)
Async XLA Ops:
  7.2 0.9 copy-start
  7.2 97.8 %copy-start.4 = (s32[1,1,128]{2,1,0:T(1,128)S(1)}, s32[1,1,128]{2,1,0:T(1,128)}, u32[]{:S(2)}) copy-start(s32[1,1,128]{2,1,0:T(1,128)} %param.16) | copy-start | bytes 1540
  7.2 97.8 %copy-start.5 = (s32[1,1,128]{2,1,0:T(1,128)S(1)}, s32[1,1,128]{2,1,0:T(1,128)}, u32[]{:S(2)}) copy-start(s32[1,1,128]{2,1,0:T(1,128)} %param.17) | copy-start | bytes 1540
  7.2 95.3 %all-gather.3.cloned.1.call-start = ((), (), s32[]{:S(2)}) async-start(), calls=%async_computation.2 | async-start | bytes 1114112 | tf_op jit(solution)/shard_map/all_gather | solution.py:56
  9.7 341.7 %reduce-scatter.3.cloned.1.call-start = ((), (), s32[]{:S(2)}) async-start(), calls=%async_computation.3 | async-start | bytes 2162688 | tf_op jit(solution)/shard_map/reduce_scatter | solution.py:59
  102.5 2.4 copy-start.1
  201.4 150.0 %copy-start.3 = (bf16[128,256]{1,0:T(8,128)(2,1)S(1)}, bf16[128,256]{1,0:T(8,128)(2,1)}, u32[]{:S(2)}) copy-start(bf16[128,256]{1,0:T(8,128)(2,1)} %param.15) | copy-start | bytes 196612
  201.4 150.0 %copy-start.6 = (f32[256]{0:T(256)S(1)}, f32[256]{0:T(256)}, u32[]{:S(2)}) copy-start(f32[256]{0:T(256)} %param.14) | copy-start | bytes 3076
  205.3 212.9 %all-gather.5.cloned.1.call-start = ((), (), s32[]{:S(2)}) async-start(), calls=%async_computation.4 | async-start | bytes 2162688 | tf_op jit(solution)/shard_map/all_gather | solution.py:65
  353.1 402.4 %reduce-scatter.5.cloned.1.call-start = ((), (), s32[]{:S(2)}) async-start(), calls=%async_computation.5 | async-start | bytes 1114112 | tf_op jit(solution)/shard_map/reduce_scatter | solution.py:68
  541.5 214.0 %copy-start.2 = (bf16[128,256]{1,0:T(8,128)(2,1)S(1)}, bf16[128,256]{1,0:T(8,128)(2,1)}, u32[]{:S(2)}) copy-start(bf16[128,256]{1,0:T(8,128)(2,1)} %param.12) | copy-start | bytes 196612
  544.2 399.8 %all-reduce.3.cloned.1.call-start = ((), (), s32[]{:S(2)}) async-start(), calls=%async_computation.6 | async-start | bytes 524288 | tf_op jit(solution)/shard_map/psum | solution.py:76
  757.2 476.5 %all-reduce.5.cloned.1.call-start = ((), (), s32[]{:S(2)}) async-start(), calls=%async_computation.7 | async-start | bytes 524288 | tf_op jit(solution)/shard_map/psum | solution.py:76
Sparse Core Ops, SparseCore 0:
  11.8 90.7 all-gather.2
  205.4 146.0 reduce-scatter.2
  354.4 63.6 all-gather.4
  544.3 211.0 reduce-scatter.4
  759.0 184.9 all-reduce.2
  946.7 286.9 all-reduce.4
